TPU v7x, 32 devices: a whole 2x2x4 slice. The times are simulated.
32 devices in a mesh: pos: 8 (over z, y), fr: 4 (over x, core).
Axes of the slice: x: 2, y: 2, z: 4, core: 2. Of those that a mesh axis runs over, the one named last changes fastest.
Arguments:
- inputs: bfloat16 [8, 2048, 1024], P('pos', 'fr'), may hold values from -6 to 6
- delays: int32 [32, 8], P('fr', 'pos'), may hold values from 0 to 2
- query_weight: bfloat16 [8, 1024, 1024], P('pos', 'fr'), may hold values from -0.1875 to 0.1875
- key_weight: bfloat16 [8, 1024, 1024], P('pos', 'fr'), may hold values from -0.1875 to 0.1875
- value_weight: bfloat16 [8, 1024, 1024], P('pos', 'fr'), may hold values from -0.1875 to 0.1875
- out_weight: bfloat16 [8, 1024, 1024], P('pos', 'fr'), may hold values from -0.375 to 0.375
- gate_weight: bfloat16 [8, 1024, 2816], P('pos', 'fr'), may hold values from -0.1875 to 0.1875
- up_weight: bfloat16 [8, 1024, 2816], P('pos', 'fr'), may hold values from -0.1875 to 0.1875
- down_weight: bfloat16 [8, 2816, 1024], P('pos', 'fr'), may hold values from -0.109375 to 0.109375
- attention_gain: bfloat16 [8, 1024], P('pos', 'fr'), may hold values from 0.099609375 to 1.8984375
- feed_gain: bfloat16 [8, 1024], P('pos', 'fr'), may hold values from 0.099609375 to 1.8984375
- cotangent: bfloat16 [8, 2048, 1024], P('pos', 'fr'), may hold values from -6 to 6
Outputs:
- output: bfloat16 [8, 2048, 1024], P('pos', 'fr')
- input_grad: bfloat16 [8, 2048, 1024], P('pos', 'fr')
- query_weight_grad: float32 [8, 1024, 1024], P('pos', 'fr')
- key_weight_grad: float32 [8, 1024, 1024], P('pos', 'fr')
- value_weight_grad: float32 [8, 1024, 1024], P('pos', 'fr')
- out_weight_grad: float32 [8, 1024, 1024], P('pos', 'fr')
- gate_weight_grad: float32 [8, 1024, 2816], P('pos', 'fr')
- up_weight_grad: float32 [8, 1024, 2816], P('pos', 'fr')
- down_weight_grad: float32 [8, 2816, 1024], P('pos', 'fr')
- attention_gain_grad: float32 [8, 1024], P('pos', 'fr')
- feed_gain_grad: float32 [8, 1024], P('pos', 'fr')
All inputs are finite; a program needn't handle non-finite values.
Results may differ from a plain program's by a relative error of at most 0.02.
Values may be sent and summed in bfloat16 or wider, within the bound.
A program may use at most 256 MiB of HBM per device.

v0:
```python
import jax
import jax.numpy as jnp
from jax import lax
from jax.sharding import PartitionSpec as P

HEAD = 64
EPSILON = 1e-06
NEGATIVE = -1e30


def shifted(x, axis, by):
    peers = lax.axis_size(axis)
    pairs = [(i, i + by) for i in range(peers) if 0 <= i + by < peers]
    return lax.ppermute(x, axis, pairs)


def rms_scaling(values):
    return lax.rsqrt(jnp.mean(values * values, -1, keepdims=True) + EPSILON)


def product(operand, weight):
    return jnp.dot(operand, weight, preferred_element_type=jnp.float32)


def outer_sum(operand, second):
    return lax.dot_general(
        operand, second, (((0,), (0,)), ((), ())), preferred_element_type=jnp.float32
    )


def back_product(grad_rows, weight):
    return lax.dot_general(
        grad_rows, weight, (((1,), (1,)), ((), ())), preferred_element_type=jnp.float32
    )


def norm_back(values, scaling, gain_row, grad_normed):
    weighted = gain_row * grad_normed
    return scaling * weighted - values * scaling**3 * jnp.mean(weighted * values, -1, keepdims=True)


def project_in(hidden, weights):
    scaling = rms_scaling(hidden)
    normed = (hidden * scaling * weights[7].astype(jnp.float32)).astype(jnp.bfloat16)
    queries = product(normed, weights[0]).astype(jnp.bfloat16)
    key_rows = product(normed, weights[1]).astype(jnp.bfloat16)
    value_rows = product(normed, weights[2]).astype(jnp.bfloat16)
    return (scaling, normed, queries, key_rows, value_rows)


def attend(queries, keys_all, values_all, position, logsum):
    frames = queries.shape[0]
    head_count = queries.shape[1] // HEAD
    positions = keys_all.shape[0]
    query_heads = queries.reshape(frames, head_count, HEAD)
    key_heads = keys_all.reshape(positions, frames, head_count, HEAD)
    value_heads = values_all.reshape(positions, frames, head_count, HEAD)
    scores = jnp.einsum(
        "fhe,jfhe->fhj", query_heads, key_heads, preferred_element_type=jnp.float32
    ) * HEAD ** (-0.5)
    allowed = jnp.arange(positions) <= position
    scores = jnp.where(allowed, scores, NEGATIVE)
    if logsum is None:
        highest = jnp.max(scores, -1, keepdims=True)
        logsum = highest + jnp.log(jnp.sum(jnp.exp(scores - highest), -1, keepdims=True))
    soft_weights = jnp.exp(scores - logsum)
    soft_low = soft_weights.astype(jnp.bfloat16)
    attended = jnp.einsum(
        "fhj,jfhe->fhe", soft_low, value_heads, preferred_element_type=jnp.float32
    )
    attended = attended.astype(jnp.bfloat16).reshape(frames, -1)
    return (attended, logsum, soft_weights, soft_low)


def finish(hidden, attended, weights):
    branch = hidden + product(attended, weights[3])
    scaling_two = rms_scaling(branch)
    normed_two = (branch * scaling_two * weights[8].astype(jnp.float32)).astype(jnp.bfloat16)
    gate_act = product(normed_two, weights[4])
    up_act = product(normed_two, weights[5])
    inner_act = (jax.nn.silu(gate_act) * up_act).astype(jnp.bfloat16)
    return (branch, scaling_two, normed_two, gate_act, up_act, inner_act)


def on_device(
    inputs,
    delays,
    query_weight,
    key_weight,
    value_weight,
    out_weight,
    gate_weight,
    up_weight,
    down_weight,
    attention_gain,
    feed_gain,
    cotangent,
):
    position = lax.axis_index("pos")
    own_rows = inputs[0]
    frames = own_rows.shape[0]
    rim_rows = shifted(own_rows[frames - 2 :], "fr", 1)
    extended = jnp.concatenate([rim_rows, own_rows], 0)
    lag_rows = jnp.repeat(delays[:, 0], frames // delays.shape[0])[:, None]
    hidden = jnp.where(
        lag_rows == 0,
        extended[2:],
        jnp.where(lag_rows == 1, extended[1 : frames + 1], extended[:frames]),
    )
    hidden = hidden.astype(jnp.float32)
    gathered = (
        lax.all_gather(query_weight, "fr", axis=1, tiled=True),
        lax.all_gather(key_weight, "fr", axis=1, tiled=True),
        lax.all_gather(value_weight, "fr", axis=1, tiled=True),
        lax.all_gather(out_weight, "fr", axis=1, tiled=True),
        lax.all_gather(gate_weight, "fr", axis=1, tiled=True),
        lax.all_gather(up_weight, "fr", axis=1, tiled=True),
        lax.all_gather(down_weight, "fr", axis=1, tiled=True),
        lax.all_gather(attention_gain, "fr", axis=1, tiled=True),
        lax.all_gather(feed_gain, "fr", axis=1, tiled=True),
    )
    forward_weights = tuple((shard_piece[0] for shard_piece in gathered))
    scaling, normed, queries, key_rows, value_rows = project_in(hidden, forward_weights)
    keys_all, values_all = (
        lax.all_gather(key_rows[None], "pos", axis=0, tiled=True),
        lax.all_gather(value_rows[None], "pos", axis=0, tiled=True),
    )
    attended, logsum, soft_weights, soft_low = attend(queries, keys_all, values_all, position, None)
    branch, scaling_two, normed_two, gate_act, up_act, inner_act = finish(
        hidden, attended, forward_weights
    )
    output = (branch + product(inner_act, forward_weights[6])).astype(jnp.bfloat16)
    regathered = (
        lax.all_gather(query_weight, "fr", axis=1, tiled=True),
        lax.all_gather(key_weight, "fr", axis=1, tiled=True),
        lax.all_gather(value_weight, "fr", axis=1, tiled=True),
        lax.all_gather(out_weight, "fr", axis=1, tiled=True),
        lax.all_gather(gate_weight, "fr", axis=1, tiled=True),
        lax.all_gather(up_weight, "fr", axis=1, tiled=True),
        lax.all_gather(down_weight, "fr", axis=1, tiled=True),
        lax.all_gather(attention_gain, "fr", axis=1, tiled=True),
        lax.all_gather(feed_gain, "fr", axis=1, tiled=True),
    )
    backward_weights = tuple((shard_piece[0] for shard_piece in regathered))
    scaling, normed, queries, key_rows, value_rows = project_in(hidden, backward_weights)
    keys_all, values_all = (
        lax.all_gather(key_rows[None], "pos", axis=0, tiled=True),
        lax.all_gather(value_rows[None], "pos", axis=0, tiled=True),
    )
    attended, logsum, soft_weights, soft_low = attend(
        queries, keys_all, values_all, position, logsum
    )
    branch, scaling_two, normed_two, gate_act, up_act, inner_act = finish(
        hidden, attended, backward_weights
    )
    (
        query_full,
        key_full,
        value_full,
        out_full,
        gate_full,
        up_full,
        down_full,
        gain_one,
        gain_two,
    ) = backward_weights
    grad_out = cotangent[0]
    grad_inner = back_product(grad_out, down_full)
    sigmoid_gate = jax.nn.sigmoid(gate_act)
    grad_gate = (
        grad_inner * up_act * sigmoid_gate * (1.0 + gate_act * (1.0 - sigmoid_gate))
    ).astype(jnp.bfloat16)
    grad_up = (grad_inner * jax.nn.silu(gate_act)).astype(jnp.bfloat16)
    down_grad = outer_sum(inner_act, grad_out)
    gate_grad = outer_sum(normed_two, grad_gate)
    up_grad = outer_sum(normed_two, grad_up)
    grad_normed_two = back_product(grad_gate, gate_full) + back_product(grad_up, up_full)
    feed_gain_grad = jnp.sum(grad_normed_two * branch * scaling_two, 0)
    grad_branch = grad_out.astype(jnp.float32) + norm_back(
        branch, scaling_two, gain_two.astype(jnp.float32), grad_normed_two
    )
    grad_branch_low = grad_branch.astype(jnp.bfloat16)
    out_grad = outer_sum(attended, grad_branch_low)
    grad_attended = back_product(grad_branch_low, out_full).astype(jnp.bfloat16)
    head_count = queries.shape[1] // HEAD
    positions = keys_all.shape[0]
    grad_heads = grad_attended.reshape(frames, head_count, HEAD)
    query_heads = queries.reshape(frames, head_count, HEAD)
    key_heads = keys_all.reshape(positions, frames, head_count, HEAD)
    value_heads = values_all.reshape(positions, frames, head_count, HEAD)
    grad_soft = jnp.einsum(
        "fhe,jfhe->fhj", grad_heads, value_heads, preferred_element_type=jnp.float32
    )
    centre = jnp.sum(grad_soft * soft_weights, -1, keepdims=True)
    grad_scores = (soft_weights * (grad_soft - centre)).astype(jnp.bfloat16)
    grad_queries = jnp.einsum(
        "fhj,jfhe->fhe", grad_scores, key_heads, preferred_element_type=jnp.float32
    ) * HEAD ** (-0.5)
    grad_queries = grad_queries.astype(jnp.bfloat16).reshape(frames, -1)
    key_terms = jnp.einsum(
        "fhj,fhe->jfhe", grad_scores, query_heads, preferred_element_type=jnp.float32
    ) * HEAD ** (-0.5)
    value_terms = jnp.einsum(
        "fhj,fhe->jfhe", soft_low, grad_heads, preferred_element_type=jnp.float32
    )
    key_sum, value_sum = (
        lax.psum_scatter(
            key_terms.reshape(positions, frames, -1).astype(jnp.bfloat16),
            "pos",
            scatter_dimension=0,
            tiled=True,
        ).astype(jnp.float32),
        lax.psum_scatter(
            value_terms.reshape(positions, frames, -1).astype(jnp.bfloat16),
            "pos",
            scatter_dimension=0,
            tiled=True,
        ).astype(jnp.float32),
    )
    grad_keys = key_sum[0].astype(jnp.bfloat16)
    grad_values = value_sum[0].astype(jnp.bfloat16)
    query_grad = outer_sum(normed, grad_queries)
    key_grad = outer_sum(normed, grad_keys)
    value_grad = outer_sum(normed, grad_values)
    grad_normed = (
        back_product(grad_queries, query_full)
        + back_product(grad_keys, key_full)
        + back_product(grad_values, value_full)
    )
    attention_gain_grad = jnp.sum(grad_normed * hidden * scaling, 0)
    grad_hidden = grad_branch + norm_back(
        hidden, scaling, gain_one.astype(jnp.float32), grad_normed
    )
    grad_extended = jnp.pad(jnp.where(lag_rows == 0, grad_hidden, 0.0), ((2, 0), (0, 0)))
    grad_extended = grad_extended + jnp.pad(
        jnp.where(lag_rows == 1, grad_hidden, 0.0), ((1, 1), (0, 0))
    )
    grad_extended = grad_extended + jnp.pad(
        jnp.where(lag_rows == 2, grad_hidden, 0.0), ((0, 2), (0, 0))
    )
    rim_back = shifted(grad_extended[:2], "fr", -1)
    input_grad = (grad_extended[2:] + jnp.pad(rim_back, ((frames - 2, 0), (0, 0)))).astype(
        jnp.bfloat16
    )
    reduced = (
        lax.psum_scatter(
            query_grad[None].astype(jnp.bfloat16), "fr", scatter_dimension=1, tiled=True
        ).astype(jnp.float32),
        lax.psum_scatter(
            key_grad[None].astype(jnp.bfloat16), "fr", scatter_dimension=1, tiled=True
        ).astype(jnp.float32),
        lax.psum_scatter(
            value_grad[None].astype(jnp.bfloat16), "fr", scatter_dimension=1, tiled=True
        ).astype(jnp.float32),
        lax.psum_scatter(
            out_grad[None].astype(jnp.bfloat16), "fr", scatter_dimension=1, tiled=True
        ).astype(jnp.float32),
        lax.psum_scatter(
            gate_grad[None].astype(jnp.bfloat16), "fr", scatter_dimension=1, tiled=True
        ).astype(jnp.float32),
        lax.psum_scatter(
            up_grad[None].astype(jnp.bfloat16), "fr", scatter_dimension=1, tiled=True
        ).astype(jnp.float32),
        lax.psum_scatter(
            down_grad[None].astype(jnp.bfloat16), "fr", scatter_dimension=1, tiled=True
        ).astype(jnp.float32),
        lax.psum_scatter(
            attention_gain_grad[None].astype(jnp.bfloat16), "fr", scatter_dimension=1, tiled=True
        ).astype(jnp.float32),
        lax.psum_scatter(
            feed_gain_grad[None].astype(jnp.bfloat16), "fr", scatter_dimension=1, tiled=True
        ).astype(jnp.float32),
    )
    return (
        output[None],
        input_grad[None],
        reduced[0],
        reduced[1],
        reduced[2],
        reduced[3],
        reduced[4],
        reduced[5],
        reduced[6],
        reduced[7],
        reduced[8],
    )


def solution(mesh):
    return jax.shard_map(
        on_device,
        mesh=mesh,
        in_specs=(
            P("pos", "fr", None),
            P("fr", "pos"),
            P("pos", "fr", None),
            P("pos", "fr", None),
            P("pos", "fr", None),
            P("pos", "fr", None),
            P("pos", "fr", None),
            P("pos", "fr", None),
            P("pos", "fr", None),
            P("pos", "fr"),
            P("pos", "fr"),
            P("pos", "fr", None),
        ),
        out_specs=(
            P("pos", "fr", None),
            P("pos", "fr", None),
            P("pos", "fr", None),
            P("pos", "fr", None),
            P("pos", "fr", None),
            P("pos", "fr", None),
            P("pos", "fr", None),
            P("pos", "fr", None),
            P("pos", "fr", None),
            P("pos", "fr"),
            P("pos", "fr"),
        ),
        check_vma=False,
    )
```

profile of v0, /device:TPU:0, one launch (start us, length us, event | category | flops | bytes accessed | tf_op | source)
XLA Modules:
  0.0 1197.0 jit_solution(10028611180217504459)
XLA Ops:
  12.8 6.3 all_gather.44
  21.0 13.9 %all-gather.14.cloned.1.call-done = bf16[1,1024,1024]{2,1,0:T(8,128)(2,1)} async-done(((bf16[1,256,1024]{2,1,0:T(8,128)(2,1)}), bf16[1,1024,1024]{2,1,0:T(8,128)(2,1)}) %all-gather.14.cloned.1.call-update) | async-done | bytes 2097168 | tf_op jit(solution)/shard_map/all_gather | solution.py:113
  34.9 3.9 fusion.51
  38.8 20.2 %all-gather.16.cloned.1.call-done = bf16[1,1024,1024]{2,1,0:T(8,128)(2,1)} async-done(((bf16[1,256,1024]{2,1,0:T(8,128)(2,1)}), bf16[1,1024,1024]{2,1,0:T(8,128)(2,1)}) %all-gather.16.cloned.1.call-update) | async-done | bytes 2097168 | tf_op jit(solution)/shard_map/all_gather | solution.py:114
  59.0 3.9 fusion.54
  65.2 5.5 all_gather.51
  70.8 12.4 %all-gather.12.cloned.1.call-done = bf16[1,1024,1024]{2,1,0:T(8,128)(2,1)} async-done(((bf16[1,256,1024]{2,1,0:T(8,128)(2,1)}), bf16[1,1024,1024]{2,1,0:T(8,128)(2,1)}) %all-gather.12.cloned.1.call-update) | async-done | bytes 2097168 | tf_op jit(solution)/shard_map/all_gather | solution.py:112
  88.9 39.1 %all-gather.24.cloned.1.call-done = bf16[1,2816,1024]{2,1,0:T(8,128)(2,1)} async-done(((bf16[1,704,1024]{2,1,0:T(8,128)(2,1)}), bf16[1,2816,1024]{2,1,0:T(8,128)(2,1)}) %all-gather.24.cloned.1.call-update) | async-done | bytes 5767184 | tf_op jit(solution)/shard_map/all_gather | solution.py:118
  128.0 8.7 fusion
  136.7 118.4 %all-gather.26.cloned.1.call-done = bf16[4096,1024]{1,0:T(8,128)(2,1)} async-done(((bf16[512,1024]{1,0:T(8,128)(2,1)}), bf16[4096,1024]{1,0:T(8,128)(2,1)}) %all-gather.26.cloned.1.call-update) | async-done | bytes 8388624 | tf_op jit(solution)/shard_map/all_gather | solution.py:125
  255.1 11.3 copy.36
  266.4 12.2 %copy.73 = bf16[128,8,8,512]{3,2,1,0:T(8,128)(2,1)} copy(bf16[128,8,8,512]{3,1,2,0:T(8,128)(2,1)} %bitcast.166) | data formatting | bytes 16777216
  278.6 101.7 %all-gather.28.cloned.1.call-done = bf16[4096,1024]{1,0:T(8,128)(2,1)} async-done(((bf16[512,1024]{1,0:T(8,128)(2,1)}), bf16[4096,1024]{1,0:T(8,128)(2,1)}) %all-gather.28.cloned.1.call-update) | async-done | bytes 8388624 | tf_op jit(solution)/shard_map/all_gather | solution.py:126
  380.3 11.5 copy.37
  391.8 12.2 %copy.74 = bf16[128,8,8,512]{3,2,1,0:T(8,128)(2,1)} copy(bf16[128,8,8,512]{3,1,2,0:T(8,128)(2,1)} %bitcast.167) | data formatting | bytes 16777216
  404.1 5.2 multiply_reduce_fusion.3
  410.7 11.3 multiply_reduce_fusion.2
  422.0 3.3 multiply_reduce_fusion.6
  426.5 21.1 %all-gather.22.cloned.1.call-done = bf16[1,1024,2816]{2,1,0:T(8,128)(2,1)} async-done(((bf16[1,256,2816]{2,1,0:T(8,128)(2,1)}), bf16[1,1024,2816]{2,1,0:T(8,128)(2,1)}) %all-gather.22.cloned.1.call-update) | async-done | bytes 5767184 | tf_op jit(solution)/shard_map/all_gather | solution.py:117
  447.6 8.6 fusion.6
  456.3 36.3 %all-gather.20.cloned.1.call-done = bf16[1,1024,2816]{2,1,0:T(8,128)(2,1)} async-done(((bf16[1,256,2816]{2,1,0:T(8,128)(2,1)}), bf16[1,1024,2816]{2,1,0:T(8,128)(2,1)}) %all-gather.20.cloned.1.call-update) | async-done | bytes 5767184 | tf_op jit(solution)/shard_map/all_gather | solution.py:116
  492.6 12.0 multiply_convert_fusion.3
  509.3 3.4 multiply_reduce_fusion.4
  522.1 6.6 multiply_reduce_fusion.1
  531.3 7.4 multiply_convert_fusion.1
  539.7 8.4 multiply_convert_fusion
  549.1 4.5 convert_bitcast_fusion.3
  555.4 10.1 multiply_reduce_fusion
  571.5 7.8 convert_bitcast_fusion
  579.4 7.8 convert_bitcast_fusion.2
  587.3 7.8 convert_bitcast_fusion.1
  595.4 91.0 %reduce-scatter.16.cloned.1.call-done = bf16[1,512,1024]{1,2,0:T(8,128)(2,1)} async-done(((bf16[8,512,1024]{1,2,0:T(8,128)(2,1)}), bf16[1,512,1024]{1,2,0:T(8,128)(2,1)}) %reduce-scatter.16.cloned.1.call-update) | async-done | bytes 1048592 | tf_op jit(solution)/shard_map/reduce_scatter | solution.py:207
  686.4 4.5 fusion.31
  690.9 145.7 %reduce-scatter.18.cloned.1.call-done = bf16[1,512,1024]{1,2,0:T(8,128)(2,1)} async-done(((bf16[8,512,1024]{1,2,0:T(8,128)(2,1)}), bf16[1,512,1024]{1,2,0:T(8,128)(2,1)}) %reduce-scatter.18.cloned.1.call-update) | async-done | bytes 1048592 | tf_op jit(solution)/shard_map/reduce_scatter | solution.py:213
  836.6 3.4 fusion.27
  844.3 4.1 convert_bitcast_fusion.5
  848.4 4.0 convert_bitcast_fusion.4
  852.7 7.7 fusion.60
  861.9 30.5 %reduce-scatter.26.cloned.1.call-done = bf16[1,256,1024]{2,1,0:T(8,128)(2,1)} async-done(((bf16[1,1024,1024]{2,1,0:T(8,128)(2,1)}), bf16[1,256,1024]{2,1,0:T(8,128)(2,1)}) %reduce-scatter.26.cloned.1.call-update) | async-done | bytes 524304 | tf_op jit(solution)/shard_map/reduce_scatter | solution.py:255
  894.5 31.4 %reduce-scatter.20.cloned.1.call-done = bf16[1,256,1024]{2,1,0:T(8,128)(2,1)} async-done(((bf16[1,1024,1024]{2,1,0:T(8,128)(2,1)}), bf16[1,256,1024]{2,1,0:T(8,128)(2,1)}) %reduce-scatter.20.cloned.1.call-update) | async-done | bytes 524304 | tf_op jit(solution)/shard_map/reduce_scatter | solution.py:246
  928.1 55.0 %reduce-scatter.32.cloned.1.call-done = bf16[1,704,1024]{2,1,0:T(8,128)(2,1)} async-done(((bf16[1,2816,1024]{2,1,0:T(8,128)(2,1)}), bf16[1,704,1024]{2,1,0:T(8,128)(2,1)}) %reduce-scatter.32.cloned.1.call-update) | async-done | bytes 1441808 | tf_op jit(solution)/shard_map/reduce_scatter | solution.py:264
  983.1 3.3 convert_element_type.251
  986.4 53.8 %reduce-scatter.28.cloned.1.call-done = bf16[1,256,2816]{2,1,0:T(8,128)(2,1)} async-done(((bf16[1,1024,2816]{2,1,0:T(8,128)(2,1)}), bf16[1,256,2816]{2,1,0:T(8,128)(2,1)}) %reduce-scatter.28.cloned.1.call-update) | async-done | bytes 1441808 | tf_op jit(solution)/shard_map/reduce_scatter | solution.py:258
  1043.4 54.0 %reduce-scatter.30.cloned.1.call-done = bf16[1,256,2816]{2,1,0:T(8,128)(2,1)} async-done(((bf16[1,1024,2816]{2,1,0:T(8,128)(2,1)}), bf16[1,256,2816]{2,1,0:T(8,128)(2,1)}) %reduce-scatter.30.cloned.1.call-update) | async-done | bytes 1441808 | tf_op jit(solution)/shard_map/reduce_scatter | solution.py:261
  1097.4 3.3 convert_element_type.248
  1104.0 16.3 %reduce-scatter.34.cloned.1.call-done = bf16[256,1]{1,0:T(8,128)(2,1)} async-done(((bf16[1024,1]{1,0:T(8,128)(2,1)}), bf16[256,1]{1,0:T(8,128)(2,1)}) %reduce-scatter.34.cloned.1.call-update) | async-done | bytes 528
  1123.1 31.0 %reduce-scatter.22.cloned.1.call-done = bf16[1,256,1024]{2,1,0:T(8,128)(2,1)} async-done(((bf16[1,1024,1024]{2,1,0:T(8,128)(2,1)}), bf16[1,256,1024]{2,1,0:T(8,128)(2,1)}) %reduce-scatter.22.cloned.1.call-update) | async-done | bytes 524304 | tf_op jit(solution)/shard_map/reduce_scatter | solution.py:249
  1156.2 31.4 %reduce-scatter.24.cloned.1.call-done = bf16[1,256,1024]{2,1,0:T(8,128)(2,1)} async-done(((bf16[1,1024,1024]{2,1,0:T(8,128)(2,1)}), bf16[1,256,1024]{2,1,0:T(8,128)(2,1)}) %reduce-scatter.24.cloned.1.call-update) | async-done | bytes 524304 | tf_op jit(solution)/shard_map/reduce_scatter | solution.py:252
  (152 shorter events, 68.3 us)
Async XLA Ops:
  7.2 2.9 copy-start.13
  7.2 5.3 copy-start.22
  7.2 5.6 copy-start.20
  7.2 27.7 %all-gather.14.cloned.1.call-start = ((), (), s32[]{:S(2)}) async-start(), calls=%async_computation.12 | async-start | bytes 2621440 | tf_op jit(solution)/shard_map/all_gather | solution.py:113
  7.9 51.1 %all-gather.16.cloned.1.call-start = ((), (), s32[]{:S(2)}) async-start(), calls=%async_computation.13 | async-start | bytes 2621440 | tf_op jit(solution)/shard_map/all_gather | solution.py:114
  8.7 74.5 %all-gather.12.cloned.1.call-start = ((), (), s32[]{:S(2)}) async-start(), calls=%async_computation.11 | async-start | bytes 2621440 | tf_op jit(solution)/shard_map/all_gather | solution.py:112
  9.4 118.6 %all-gather.24.cloned.1.call-start = ((), (), s32[]{:S(2)}) async-start(), calls=%async_computation.17 | async-start | bytes 7208960 | tf_op jit(solution)/shard_map/all_gather | solution.py:118
  10.0 245.1 %all-gather.26.cloned.1.call-start = ((), (), s32[]{:S(2)}) async-start(), calls=%async_computation.27 | async-start | bytes 9437184 | tf_op jit(solution)/shard_map/all_gather | solution.py:125
  10.1 9.1 collective-permute-start
  12.7 26.1 %copy-start.16 = (pred[512]{0:T(512)(128)(4,1)}, pred[512]{0:T(512)(128)(4,1)S(1)}, u32[]{:S(2)}) copy-start(pred[512]{0:T(512)(128)(4,1)S(1)} %eq.52) | copy-start | bytes 1540
  12.8 25.9 %copy-start.18 = (pred[512]{0:T(512)(128)(4,1)}, pred[512]{0:T(512)(128)(4,1)S(1)}, u32[]{:S(2)}) copy-start(pred[512]{0:T(512)(128)(4,1)S(1)} %eq.55) | copy-start | bytes 1540
  38.8 341.5 %all-gather.28.cloned.1.call-start = ((), (), s32[]{:S(2)}) async-start(), calls=%async_computation.28 | async-start | bytes 9437184 | tf_op jit(solution)/shard_map/all_gather | solution.py:126
  62.9 2.3 copy-start.21
  62.9 359.1 %all-gather.18.cloned.1.call-start = ((), (), s32[]{:S(2)}) async-start(), calls=%async_computation.14 | async-start | bytes 2621440 | tf_op jit(solution)/shard_map/all_gather | solution.py:115
  63.7 384.0 %all-gather.22.cloned.1.call-start = ((), (), s32[]{:S(2)}) async-start(), calls=%async_computation.16 | async-start | bytes 7208960 | tf_op jit(solution)/shard_map/all_gather | solution.py:117
  64.4 428.2 %all-gather.20.cloned.1.call-start = ((), (), s32[]{:S(2)}) async-start(), calls=%async_computation.15 | async-start | bytes 7208960 | tf_op jit(solution)/shard_map/all_gather | solution.py:116
  65.2 621.2 %reduce-scatter.16.cloned.1.call-start = ((), (), s32[]{:S(2)}) async-start(), calls=%async_computation.18 | async-start | bytes 9437184 | tf_op jit(solution)/shard_map/reduce_scatter | solution.py:207
  88.9 315.1 %copy-start = (f32[512,16,64]{0,2,1:T(8,128)}, f32[512,16,64]{0,2,1:T(8,128)S(1)}, u32[]{:S(2)}) copy-start(f32[512,16,64]{0,2,1:T(8,128)S(1)} %bitcast_convert_fusion.1) | copy-start | bytes 6291460
  409.9 0.7 copy-start.8
  492.6 12.0 %copy-start.23 = (bf16[1,1024,2816]{2,1,0:T(8,128)(2,1)S(1)}, bf16[1,1024,2816]{2,1,0:T(8,128)(2,1)}, u32[]{:S(2)}) copy-start(bf16[1,1024,2816]{2,1,0:T(8,128)(2,1)} %all-gather.22.cloned.1.call-done) | copy-start | bytes 17301508
  504.6 3.2 copy-start.26
  504.6 3.2 copy-start.25
  504.6 4.7 copy-start.24
  509.3 3.4 copy-start.14
  512.8 1.9 copy-start.12
  513.4 1.3 copy-start.1
  531.3 7.4 copy-start.6
  538.7 1.0 copy-start.9
  538.7 297.9 %reduce-scatter.18.cloned.1.call-start = ((), (), s32[]{:S(2)}) async-start(), calls=%async_computation.19 | async-start | bytes 9437184 | tf_op jit(solution)/shard_map/reduce_scatter | solution.py:213
  548.0 312.3 %reduce-scatter.36.cloned.1.call-start = ((), (), s32[]{:S(2)}) async-start(), calls=%async_computation.30 | async-start | bytes 327680
  549.0 343.4 %reduce-scatter.26.cloned.1.call-start = ((), (), s32[]{:S(2)}) async-start(), calls=%async_computation.23 | async-start | bytes 2621440 | tf_op jit(solution)/shard_map/reduce_scatter | solution.py:255
  553.6 1.0 copy-start.7
  553.6 372.3 %reduce-scatter.20.cloned.1.call-start = ((), (), s32[]{:S(2)}) async-start(), calls=%async_computation.20 | async-start | bytes 2621440 | tf_op jit(solution)/shard_map/reduce_scatter | solution.py:246
  567.4 1.0 copy-start.4
  571.2 411.9 %reduce-scatter.32.cloned.1.call-start = ((), (), s32[]{:S(2)}) async-start(), calls=%async_computation.26 | async-start | bytes 7208960 | tf_op jit(solution)/shard_map/reduce_scatter | solution.py:264
  579.3 461.0 %reduce-scatter.28.cloned.1.call-start = ((), (), s32[]{:S(2)}) async-start(), calls=%async_computation.24 | async-start | bytes 7208960 | tf_op jit(solution)/shard_map/reduce_scatter | solution.py:258
  587.2 510.2 %reduce-scatter.30.cloned.1.call-start = ((), (), s32[]{:S(2)}) async-start(), calls=%async_computation.25 | async-start | bytes 7208960 | tf_op jit(solution)/shard_map/reduce_scatter | solution.py:261
  595.1 525.2 %reduce-scatter.34.cloned.1.call-start = ((), (), s32[]{:S(2)}) async-start(), calls=%async_computation.29 | async-start | bytes 327680
  836.6 3.4 copy-start.5
  836.6 3.4 copy-start.10
  836.6 3.5 copy-start.11
  844.2 309.8 %reduce-scatter.22.cloned.1.call-start = ((), (), s32[]{:S(2)}) async-start(), calls=%async_computation.21 | async-start | bytes 2621440 | tf_op jit(solution)/shard_map/reduce_scatter | solution.py:249
  848.4 339.2 %reduce-scatter.24.cloned.1.call-start = ((), (), s32[]{:S(2)}) async-start(), calls=%async_computation.22 | async-start | bytes 2621440 | tf_op jit(solution)/shard_map/reduce_scatter | solution.py:252
  1043.4 57.3 %copy-start.2 = (f32[512,1024]{1,0:T(8,128)S(1)}, f32[512,1024]{1,0:T(8,128)}, u32[]{:S(2)}) copy-start(f32[512,1024]{1,0:T(8,128)} %copy-done.1) | copy-start | bytes 6291460
  1043.4 57.3 %copy-start.15 = (f32[512]{0:T(512)S(1)}, f32[512]{0:T(512)}, u32[]{:S(2)}) copy-start(f32[512]{0:T(512)} %get-tuple-element.24) | copy-start | bytes 6148
  1043.4 57.3 %copy-start.17 = (pred[512]{0:T(512)(128)(4,1)S(1)}, pred[512]{0:T(512)(128)(4,1)}, u32[]{:S(2)}) copy-start(pred[512]{0:T(512)(128)(4,1)} %copy-done.16) | copy-start | bytes 1540
  1097.4 3.3 copy-start.3
  1101.8 20.1 %collective-permute-start.1 = (f32[2,1024]{1,0:T(2,128)S(1)}, f32[2,1024]{1,0:T(2,128)S(1)}, u32[]{:S(2)}, u32[]{:S(2)}) collective-permute-start(f32[2,1024]{1,0:T(2,128)S(1)} %pad_add_fusion.1), channel_id=1, source_target_pairs={{1,0},{2,1},{3,2},{5,4},{6,5},{7,6},{9,8},{10,9},{11,10},{13,12},{... | collective-permute-start | bytes 24584 | tf_op jit(solution)/shard_map/ppermute | solution.py:14
  (1 other events, 0.7 us)
Sparse Core Ops, SparseCore 0:
  9.6 25.2 all-gather.13
  36.4 22.5 all-gather.15
  60.6 22.5 all-gather.11
  84.6 43.3 all-gather.23
  130.6 124.4 all-gather.25
  257.6 122.6 all-gather.27
  381.9 20.7 all-gather.17
  404.2 43.3 all-gather.21
  449.2 43.3 all-gather.19
  538.9 147.4 reduce-scatter.15
  690.0 146.5 reduce-scatter.17
  839.5 19.1 reduce-scatter.35
  861.2 31.1 reduce-scatter.25
  894.8 31.1 reduce-scatter.19
  928.4 54.7 reduce-scatter.31
  985.5 54.7 reduce-scatter.27
  1042.6 54.7 reduce-scatter.29
  1100.3 20.0 reduce-scatter.33
  1122.9 31.1 reduce-scatter.21
  1156.4 31.1 reduce-scatter.23
where the time goes:
time: 1200 us
  waiting for transfers between devices  908 us (76%)
  matrix products  110 us (9%)
  other arithmetic  84.5 us (7%)
  local copies, waits for them, and re-layouts  62.3 us (5%)
  between operations  15.2 us (1%)
    reduce_scatter x1, waiting for transfers between devices, on_device(): lax.psum_scatter(value_terms.reshape(positions, frames, -1).astype(jnp.bf...  146 us
    all_gather x1, waiting for transfers between devices, on_device(): lax.all_gather(key_rows[None], 'pos', axis=0, tiled=True)  118 us
    all_gather x1, waiting for transfers between devices, on_device(): lax.all_gather(value_rows[None], 'pos', axis=0, tiled=True)  102 us
    reduce_scatter x1, waiting for transfers between devices, on_device(): lax.psum_scatter(key_terms.reshape(positions, frames, -1).astype(jnp.bflo...  91 us
    reduce_scatter x1, waiting for transfers between devices, on_device(): lax.psum_scatter(down_grad[None].astype(jnp.bfloat16), 'fr', scatter_dime...  55 us
    reduce_scatter x1, waiting for transfers between devices, on_device(): lax.psum_scatter(up_grad[None].astype(jnp.bfloat16), 'fr', scatter_dimens...  54 us
    reduce_scatter x1, waiting for transfers between devices, on_device(): lax.psum_scatter(gate_grad[None].astype(jnp.bfloat16), 'fr', scatter_dime...  53.8 us
    dot_general x7, matrix products, product(): return jnp.dot(operand, weight, preferred_element_type=jnp.float32)  42.2 us
  transfers between devices with their start and end apart: 22, of which 18 were waited for; matrix products, arithmetic and copies ran while one was open for 17% of the time, Pallas kernels for 0%

commit v1 on v0

--- a/solution.py
+++ b/solution.py
@@ -6,6 +6,27 @@
 HEAD = 64
 EPSILON = 1e-06
 NEGATIVE = -1e30
+
+
+def collect(array, axis, dim):
+    length, place, rows = (lax.axis_size(axis), lax.axis_index(axis), array.shape[dim])
+    right = [(i, (i + 1) % length) for i in range(length)]
+    downward = [(i, (i - 1) % length) for i in range(length)]
+    whole = jnp.zeros((*array.shape[:dim], length * rows, *array.shape[dim + 1 :]), array.dtype)
+    whole = lax.dynamic_update_slice_in_dim(whole, array, place * rows, axis=dim)
+    from_left = from_right = array
+    half = length // 2
+    for turn in range(1, half + 1):
+        from_left = lax.ppermute(from_left, axis, right)
+        whole = lax.dynamic_update_slice_in_dim(
+            whole, from_left, (place - turn) % length * rows, axis=dim
+        )
+        if turn < length - half:
+            from_right = lax.ppermute(from_right, axis, downward)
+            whole = lax.dynamic_update_slice_in_dim(
+                whole, from_right, (place + turn) % length * rows, axis=dim
+            )
+    return whole
 
 
 def shifted(x, axis, by):
@@ -122,7 +143,7 @@
     forward_weights = tuple((shard_piece[0] for shard_piece in gathered))
     scaling, normed, queries, key_rows, value_rows = project_in(hidden, forward_weights)
     keys_all, values_all = (
-        lax.all_gather(key_rows[None], "pos", axis=0, tiled=True),
+        collect(key_rows[None], "pos", 0),
         lax.all_gather(value_rows[None], "pos", axis=0, tiled=True),
     )
     attended, logsum, soft_weights, soft_low = attend(queries, keys_all, values_all, position, None)

time: 1200 us -> 1250 us (1.042)
  local copies, waits for them, and re-layouts: 62.3 us -> 107 us
  waiting for transfers between devices: 908 us -> 876 us
  starting transfers between devices: 5.13 us -> 23.5 us
  matrix products: 110 us -> 126 us
    ppermute x0 -> x7, waiting for transfers between devices: none -> 155 us  [the longest x4 155 us: collect(): from_left = lax.ppermute(from_left, axis, right)]
    all_gather x1, waiting for transfers between devices: 118 us -> 16.8 us  [on_device(): lax.all_gather(key_rows[None], 'pos', axis=0, tiled=True)]
    reduce_scatter x1, waiting for transfers between devices: 146 us -> 84.3 us  [on_device(): lax.psum_scatter(value_terms.reshape(positions, frames, -1).astype(jnp.bf...]
    reduce_scatter x1, waiting for transfers between devices: 91 us -> 146 us  [on_device(): lax.psum_scatter(key_terms.reshape(positions, frames, -1).astype(jnp.bflo...]
    all_gather x1, waiting for transfers between devices: 39.1 us -> 0.02 us  [on_device(): lax.all_gather(down_weight, 'fr', axis=1, tiled=True)]
    reduce_scatter x1, waiting for transfers between devices: 31.4 us -> 12.5 us  [on_device(): lax.psum_scatter(query_grad[None].astype(jnp.bfloat16), 'fr', scatter_dim...]
    ppermute x0 -> x7, starting transfers between devices: none -> 18.2 us  [the longest x4 9.24 us: collect(): from_left = lax.ppermute(from_left, axis, right)]
    dot_general x7 -> x9, matrix products: 42.2 us -> 60.1 us  [product(): return jnp.dot(operand, weight, preferred_element_type=jnp.float32)]
  transfers between devices with their start and end apart: 22 -> 29, of which waited for: 18 -> 20; matrix products, arithmetic and copies ran while one was open for 17% -> 22% of each run, Pallas kernels for 0% -> 0%
where the time goes in v1:
time: 1250 us
  waiting for transfers between devices  876 us (70%)
  matrix products  126 us (10%)
  local copies, waits for them, and re-layouts  107 us (9%)
  other arithmetic  88.9 us (7%)
  starting transfers between devices  23.5 us (2%)
  between operations  15.1 us (1%)
    ppermute x4, waiting for transfers between devices, collect(): from_left = lax.ppermute(from_left, axis, right)  155 us
    reduce_scatter x1, waiting for transfers between devices, on_device(): lax.psum_scatter(key_terms.reshape(positions, frames, -1).astype(jnp.bflo...  146 us
    all_gather x1, waiting for transfers between devices, on_device(): lax.all_gather(value_rows[None], 'pos', axis=0, tiled=True)  91.6 us
    reduce_scatter x1, waiting for transfers between devices, on_device(): lax.psum_scatter(value_terms.reshape(positions, frames, -1).astype(jnp.bf...  84.3 us
    dot_general x9, matrix products, product(): return jnp.dot(operand, weight, preferred_element_type=jnp.float32)  60.1 us
    reduce_scatter x1, waiting for transfers between devices, on_device(): lax.psum_scatter(gate_grad[None].astype(jnp.bfloat16), 'fr', scatter_dime...  55 us
    reduce_scatter x1, waiting for transfers between devices, on_device(): lax.psum_scatter(up_grad[None].astype(jnp.bfloat16), 'fr', scatter_dimens...  54 us
    reduce_scatter x1, waiting for transfers between devices, on_device(): lax.psum_scatter(down_grad[None].astype(jnp.bfloat16), 'fr', scatter_dime...  54 us
  transfers between devices with their start and end apart: 29, of which 20 were waited for; matrix products, arithmetic and copies ran while one was open for 22% of the time, Pallas kernels for 0%

profile of v1, /device:TPU:0, one launch (start us, length us, event | category | flops | bytes accessed | tf_op | source)
XLA Modules:
  0.0 1248.2 jit_solution(2889916876945914929)
XLA Ops:
  13.3 6.3 all_gather.43
  21.4 13.4 %all-gather.14.cloned.1.call-done = bf16[1,1024,1024]{2,1,0:T(8,128)(2,1)} async-done(((bf16[1,256,1024]{2,1,0:T(8,128)(2,1)}), bf16[1,1024,1024]{2,1,0:T(8,128)(2,1)}) %all-gather.14.cloned.1.call-update) | async-done | bytes 2097168 | tf_op jit(solution)/shard_map/all_gather | solution.py:134
  34.9 3.9 fusion.63
  38.8 20.2 %all-gather.16.cloned.1.call-done = bf16[1,1024,1024]{2,1,0:T(8,128)(2,1)} async-done(((bf16[1,256,1024]{2,1,0:T(8,128)(2,1)}), bf16[1,1024,1024]{2,1,0:T(8,128)(2,1)}) %all-gather.16.cloned.1.call-update) | async-done | bytes 2097168 | tf_op jit(solution)/shard_map/all_gather | solution.py:135
  59.0 3.9 fusion.66
  69.3 42.0 %collective-permute-done.1 = bf16[1,512,1024]{2,1,0:T(8,128)(2,1)} collective-permute-done((bf16[1,512,1024]{2,1,0:T(8,128)(2,1)S(1)}, bf16[1,512,1024]{2,1,0:T(8,128)(2,1)}, u32[]{:S(2)}, u32[]{:S(2)}) %collective-permute-start.1) | collective-permute-done | bytes 1048608 | tf_op jit(solution)/shard_map/ppermute | solution.py:20
  116.8 53.0 %collective-permute-done.3 = bf16[1,512,1024]{2,1,0:T(8,128)(2,1)S(1)} collective-permute-done((bf16[1,512,1024]{2,1,0:T(8,128)(2,1)}, bf16[1,512,1024]{2,1,0:T(8,128)(2,1)S(1)}, u32[]{:S(2)}, u32[]{:S(2)}) %collective-permute-start.3) | collective-permute-done | bytes 1048608 | tf_op jit(solution)/shard_map/ppermute | solution.py:20
  172.2 5.1 all_gather.49
  184.4 48.5 %collective-permute-done.5 = bf16[1,512,1024]{2,1,0:T(8,128)(2,1)} collective-permute-done((bf16[1,512,1024]{2,1,0:T(8,128)(2,1)S(1)}, bf16[1,512,1024]{2,1,0:T(8,128)(2,1)}, u32[]{:S(2)}, u32[]{:S(2)}) %collective-permute-start.5) | collective-permute-done | bytes 1048608 | tf_op jit(solution)/shard_map/ppermute | solution.py:20
  239.4 4.0 broadcast_in_dim.96
  268.4 11.1 collective-permute-done.7
  284.1 6.3 multiply_reduce_fusion.3
  291.3 8.9 fusion.2
  300.1 16.8 %all-gather.28.cloned.1.call-done = bf16[4096,1024]{1,0:T(8,128)(2,1)} async-done(((bf16[512,1024]{1,0:T(8,128)(2,1)}), bf16[4096,1024]{1,0:T(8,128)(2,1)}) %all-gather.28.cloned.1.call-update) | async-done | bytes 8388624 | tf_op jit(solution)/shard_map/all_gather | solution.py:168
  316.9 12.3 copy.61
  329.1 12.3 copy.111
  341.4 5.3 multiply_reduce_fusion.2
  350.1 91.6 %all-gather.26.cloned.1.call-done = bf16[4096,1024]{1,0:T(8,128)(2,1)} async-done(((bf16[512,1024]{1,0:T(8,128)(2,1)}), bf16[4096,1024]{1,0:T(8,128)(2,1)}) %all-gather.26.cloned.1.call-update) | async-done | bytes 8388624 | tf_op jit(solution)/shard_map/all_gather | solution.py:147
  441.7 12.4 copy.60
  454.1 12.3 copy.110
  466.6 13.9 %fusion.1 = (bf16[512,16,64]{0,2,1:T(8,128)(2,1)}, bf16[512,16,64]{0,2,1:T(8,128)(2,1)}) fusion(f32[512,16,8]{0,2,1:T(8,128)S(1)} %copy-done.26, bf16[8,512,16,64]{1,0,3,2:T(8,128)(2,1)} %bitcast.187, f32[512,16,8]{0,2,1:T(8,128)S(1)} %copy.105), kind=kLoop, calls=%fused_computation.3 | loop fusion | flops 19922944 | bytes 11010048 | tf_op jit(solution)/shard_map/fhj,jfhe->fhe/dot_general | solution.py:89
  486.4 22.6 %all-gather.22.cloned.1.call-done = bf16[1,1024,2816]{2,1,0:T(8,128)(2,1)} async-done(((bf16[1,256,2816]{2,1,0:T(8,128)(2,1)}), bf16[1,1024,2816]{2,1,0:T(8,128)(2,1)}) %all-gather.22.cloned.1.call-update) | async-done | bytes 5767184 | tf_op jit(solution)/shard_map/all_gather | solution.py:138
  509.0 8.6 fusion.8
  517.6 36.3 %all-gather.20.cloned.1.call-done = bf16[1,1024,2816]{2,1,0:T(8,128)(2,1)} async-done(((bf16[1,256,2816]{2,1,0:T(8,128)(2,1)}), bf16[1,1024,2816]{2,1,0:T(8,128)(2,1)}) %all-gather.20.cloned.1.call-update) | async-done | bytes 5767184 | tf_op jit(solution)/shard_map/all_gather | solution.py:137
  554.0 11.7 multiply_convert_fusion.4
  582.8 6.7 multiply_convert_fusion
  589.5 6.6 multiply_reduce_fusion.1
  598.8 5.8 multiply_convert_fusion.1
  606.6 8.7 multiply_reduce_fusion
  616.6 4.0 convert_bitcast_fusion.6
  622.3 3.8 convert_bitcast_fusion.3
  627.3 6.8 convert_bitcast_fusion.2
  634.2 7.0 convert_bitcast_fusion.1
  642.5 10.3 convert_bitcast_fusion
  652.8 84.3 %reduce-scatter.18.cloned.1.call-done = bf16[1,512,1024]{1,2,0:T(8,128)(2,1)} async-done(((bf16[8,512,1024]{1,2,0:T(8,128)(2,1)}), bf16[1,512,1024]{1,2,0:T(8,128)(2,1)}) %reduce-scatter.18.cloned.1.call-update) | async-done | bytes 1048592 | tf_op jit(solution)/shard_map/reduce_scatter | solution.py:234
  737.1 3.8 fusion.37
  741.0 146.4 %reduce-scatter.16.cloned.1.call-done = bf16[1,512,1024]{1,2,0:T(8,128)(2,1)} async-done(((bf16[8,512,1024]{1,2,0:T(8,128)(2,1)}), bf16[1,512,1024]{1,2,0:T(8,128)(2,1)}) %reduce-scatter.16.cloned.1.call-update) | async-done | bytes 1048592 | tf_op jit(solution)/shard_map/reduce_scatter | solution.py:228
  899.4 3.9 multiply_reduce_fusion.7
  907.7 7.8 fusion.16
  915.5 14.2 %fusion.76 = bf16[1,512,1024]{2,1,0:T(8,128)(2,1)} fusion(f32[512,1024]{1,0:T(8,128)S(1)} %copy-done.22, bf16[1,2816,1024]{2,1,0:T(8,128)(2,1)} %all-gather.24.cloned.1.call-done, f32[512,2816]{1,0:T(8,128)} %fusion.16, bf16[1,1024,2816]{2,1,0:T(8,128)(2,1)} %all-gather.22.cloned.1.call-done, f32[1024]{0:T(1024)S(1)} %bitcast.216, f32[512]{0:T(512)S(1)} %add_rsqrt_fusion.1), kind=kOutput, calls=%fused_computation.91 | convolution fusion | flops 5916852224 | bytes 20453376 | tf_op jit(solution)/shard_map/dot_general | solution.py:43
  931.2 12.5 %reduce-scatter.20.cloned.1.call-done = bf16[1,256,1024]{2,1,0:T(8,128)(2,1)} async-done(((bf16[1,1024,1024]{2,1,0:T(8,128)(2,1)}), bf16[1,256,1024]{2,1,0:T(8,128)(2,1)}) %reduce-scatter.20.cloned.1.call-update) | async-done | bytes 524304 | tf_op jit(solution)/shard_map/reduce_scatter | solution.py:267
  945.8 31.4 %reduce-scatter.26.cloned.1.call-done = bf16[1,256,1024]{2,1,0:T(8,128)(2,1)} async-done(((bf16[1,1024,1024]{2,1,0:T(8,128)(2,1)}), bf16[1,256,1024]{2,1,0:T(8,128)(2,1)}) %reduce-scatter.26.cloned.1.call-update) | async-done | bytes 524304 | tf_op jit(solution)/shard_map/reduce_scatter | solution.py:276
  979.4 55.0 %reduce-scatter.28.cloned.1.call-done = bf16[1,256,2816]{2,1,0:T(8,128)(2,1)} async-done(((bf16[1,1024,2816]{2,1,0:T(8,128)(2,1)}), bf16[1,256,2816]{2,1,0:T(8,128)(2,1)}) %reduce-scatter.28.cloned.1.call-update) | async-done | bytes 1441808 | tf_op jit(solution)/shard_map/reduce_scatter | solution.py:279
  1037.5 54.0 %reduce-scatter.30.cloned.1.call-done = bf16[1,256,2816]{2,1,0:T(8,128)(2,1)} async-done(((bf16[1,1024,2816]{2,1,0:T(8,128)(2,1)}), bf16[1,256,2816]{2,1,0:T(8,128)(2,1)}) %reduce-scatter.30.cloned.1.call-update) | async-done | bytes 1441808 | tf_op jit(solution)/shard_map/reduce_scatter | solution.py:282
  1094.7 54.0 %reduce-scatter.32.cloned.1.call-done = bf16[1,704,1024]{2,1,0:T(8,128)(2,1)} async-done(((bf16[1,2816,1024]{2,1,0:T(8,128)(2,1)}), bf16[1,704,1024]{2,1,0:T(8,128)(2,1)}) %reduce-scatter.32.cloned.1.call-update) | async-done | bytes 1441808 | tf_op jit(solution)/shard_map/reduce_scatter | solution.py:285
  1155.5 16.2 %reduce-scatter.34.cloned.1.call-done = bf16[256,1]{1,0:T(8,128)(2,1)} async-done(((bf16[1024,1]{1,0:T(8,128)(2,1)}), bf16[256,1]{1,0:T(8,128)(2,1)}) %reduce-scatter.34.cloned.1.call-update) | async-done | bytes 528
  1174.4 31.0 %reduce-scatter.22.cloned.1.call-done = bf16[1,256,1024]{2,1,0:T(8,128)(2,1)} async-done(((bf16[1,1024,1024]{2,1,0:T(8,128)(2,1)}), bf16[1,256,1024]{2,1,0:T(8,128)(2,1)}) %reduce-scatter.22.cloned.1.call-update) | async-done | bytes 524304 | tf_op jit(solution)/shard_map/reduce_scatter | solution.py:270
  1207.5 31.5 %reduce-scatter.24.cloned.1.call-done = bf16[1,256,1024]{2,1,0:T(8,128)(2,1)} async-done(((bf16[1,1024,1024]{2,1,0:T(8,128)(2,1)}), bf16[1,256,1024]{2,1,0:T(8,128)(2,1)}) %reduce-scatter.24.cloned.1.call-update) | async-done | bytes 524304 | tf_op jit(solution)/shard_map/reduce_scatter | solution.py:273
  (226 shorter events, 145.0 us)
Async XLA Ops:
  7.2 5.3 copy-start.37
  7.2 6.1 copy-start.35
  7.2 27.7 %all-gather.14.cloned.1.call-start = ((), (), s32[]{:S(2)}) async-start(), calls=%async_computation.12 | async-start | bytes 2621440 | tf_op jit(solution)/shard_map/all_gather | solution.py:134
  7.9 51.1 %all-gather.16.cloned.1.call-start = ((), (), s32[]{:S(2)}) async-start(), calls=%async_computation.13 | async-start | bytes 2621440 | tf_op jit(solution)/shard_map/all_gather | solution.py:135
  8.7 171.5 %all-gather.12.cloned.1.call-start = ((), (), s32[]{:S(2)}) async-start(), calls=%async_computation.11 | async-start | bytes 2621440 | tf_op jit(solution)/shard_map/all_gather | solution.py:133
  9.4 281.8 %all-gather.24.cloned.1.call-start = ((), (), s32[]{:S(2)}) async-start(), calls=%async_computation.17 | async-start | bytes 7208960 | tf_op jit(solution)/shard_map/all_gather | solution.py:139
  10.0 306.9 %all-gather.28.cloned.1.call-start = ((), (), s32[]{:S(2)}) async-start(), calls=%async_computation.28 | async-start | bytes 9437184 | tf_op jit(solution)/shard_map/all_gather | solution.py:168
  10.1 9.6 collective-permute-start
  13.2 25.6 %copy-start.33 = (pred[512]{0:T(512)(128)(4,1)}, pred[512]{0:T(512)(128)(4,1)S(1)}, u32[]{:S(2)}) copy-start(pred[512]{0:T(512)(128)(4,1)S(1)} %eq.63) | copy-start | bytes 1540
  13.3 25.4 %copy-start.31 = (pred[512]{0:T(512)(128)(4,1)}, pred[512]{0:T(512)(128)(4,1)S(1)}, u32[]{:S(2)}) copy-start(pred[512]{0:T(512)(128)(4,1)S(1)} %eq.60) | copy-start | bytes 1540
  38.8 402.9 %all-gather.26.cloned.1.call-start = ((), (), s32[]{:S(2)}) async-start(), calls=%async_computation.27 | async-start | bytes 9437184 | tf_op jit(solution)/shard_map/all_gather | solution.py:147
  62.9 109.3 %copy-start.36 = (bf16[1,256]{1,0:T(2,128)(2,1)S(1)}, bf16[1,256]{1,0:T(2,128)(2,1)}, u32[]{:S(2)}) copy-start(bf16[1,256]{1,0:T(2,128)(2,1)} %param.22) | copy-start | bytes 1540
  62.9 417.6 %all-gather.18.cloned.1.call-start = ((), (), s32[]{:S(2)}) async-start(), calls=%async_computation.14 | async-start | bytes 2621440 | tf_op jit(solution)/shard_map/all_gather | solution.py:136
  63.7 445.3 %all-gather.22.cloned.1.call-start = ((), (), s32[]{:S(2)}) async-start(), calls=%async_computation.16 | async-start | bytes 7208960 | tf_op jit(solution)/shard_map/all_gather | solution.py:138
  64.4 489.5 %all-gather.20.cloned.1.call-start = ((), (), s32[]{:S(2)}) async-start(), calls=%async_computation.15 | async-start | bytes 7208960 | tf_op jit(solution)/shard_map/all_gather | solution.py:137
  64.5 46.8 %collective-permute-start.1 = (bf16[1,512,1024]{2,1,0:T(8,128)(2,1)S(1)}, bf16[1,512,1024]{2,1,0:T(8,128)(2,1)}, u32[]{:S(2)}, u32[]{:S(2)}) collective-permute-start(bf16[1,512,1024]{2,1,0:T(8,128)(2,1)S(1)} %bitcast.196), channel_id=1, source_target_pairs={{0,4},{4,8},{8,12},{12,16},{16,20},{20,24},{24,28},{28,0},{1,5},{5... | collective-permute-start | bytes 3145736 | tf_op jit(solution)/shard_map/ppermute | solution.py:20
  66.0 47.9 %collective-permute-start.2 = (bf16[1,512,1024]{2,1,0:T(8,128)(2,1)S(1)}, bf16[1,512,1024]{2,1,0:T(8,128)(2,1)}, u32[]{:S(2)}, u32[]{:S(2)}) collective-permute-start(bf16[1,512,1024]{2,1,0:T(8,128)(2,1)S(1)} %bitcast.197), channel_id=1, source_target_pairs={{0,28},{4,0},{8,4},{12,8},{16,12},{20,16},{24,20},{28,24},{1,29},{... | collective-permute-start | bytes 3145736 | tf_op jit(solution)/shard_map/ppermute | solution.py:25
  111.3 58.5 %collective-permute-start.3 = (bf16[1,512,1024]{2,1,0:T(8,128)(2,1)}, bf16[1,512,1024]{2,1,0:T(8,128)(2,1)S(1)}, u32[]{:S(2)}, u32[]{:S(2)}) collective-permute-start(bf16[1,512,1024]{2,1,0:T(8,128)(2,1)} %collective-permute-done.1), channel_id=1, source_target_pairs={{0,4},{4,8},{8,12},{12,16},{16,20},{20,24},{24,28},{28,0},{1,5},{5... | collective-permute-start | bytes 3145736 | tf_op jit(solution)/shard_map/ppermute | solution.py:20
  113.9 623.2 %reduce-scatter.18.cloned.1.call-start = ((), (), s32[]{:S(2)}) async-start(), calls=%async_computation.19 | async-start | bytes 9437184 | tf_op jit(solution)/shard_map/reduce_scatter | solution.py:234
  114.0 63.3 %collective-permute-start.4 = (bf16[1,512,1024]{2,1,0:T(8,128)(2,1)}, bf16[1,512,1024]{2,1,0:T(8,128)(2,1)}, u32[]{:S(2)}, u32[]{:S(2)}) collective-permute-start(bf16[1,512,1024]{2,1,0:T(8,128)(2,1)} %collective-permute-done.2), channel_id=1, source_target_pairs={{0,28},{4,0},{8,4},{12,8},{16,12},{20,16},{24,20},{28,24},{1,29},{... | collective-permute-start | bytes 3145736 | tf_op jit(solution)/shard_map/ppermute | solution.py:25
  169.8 13.2 %copy-start.27 = (bf16[1,512,1024]{2,1,0:T(8,128)(2,1)}, bf16[1,512,1024]{2,1,0:T(8,128)(2,1)S(1)}, u32[]{:S(2)}) copy-start(bf16[1,512,1024]{2,1,0:T(8,128)(2,1)S(1)} %collective-permute-done.3) | copy-start | bytes 3145732
  169.8 63.1 %collective-permute-start.5 = (bf16[1,512,1024]{2,1,0:T(8,128)(2,1)S(1)}, bf16[1,512,1024]{2,1,0:T(8,128)(2,1)}, u32[]{:S(2)}, u32[]{:S(2)}) collective-permute-start(bf16[1,512,1024]{2,1,0:T(8,128)(2,1)S(1)} %collective-permute-done.3), channel_id=1, source_target_pairs={{0,4},{4,8},{8,12},{12,16},{16,20},{20,24},{24,28},{28,0},{1,5},{5... | collective-permute-start | bytes 3145736 | tf_op jit(solution)/shard_map/ppermute | solution.py:20
  177.3 85.5 %collective-permute-start.6 = (bf16[1,512,1024]{2,1,0:T(8,128)(2,1)}, bf16[1,512,1024]{2,1,0:T(8,128)(2,1)}, u32[]{:S(2)}, u32[]{:S(2)}) collective-permute-start(bf16[1,512,1024]{2,1,0:T(8,128)(2,1)} %collective-permute-done.4), channel_id=1, source_target_pairs={{0,28},{4,0},{8,4},{12,8},{16,12},{20,16},{24,20},{28,24},{1,29},{... | collective-permute-start | bytes 3145736 | tf_op jit(solution)/shard_map/ppermute | solution.py:25
  232.9 46.6 %collective-permute-start.7 = (bf16[1,512,1024]{2,1,0:T(8,128)(2,1)}, bf16[1,512,1024]{2,1,0:T(8,128)(2,1)}, u32[]{:S(2)}, u32[]{:S(2)}) collective-permute-start(bf16[1,512,1024]{2,1,0:T(8,128)(2,1)} %collective-permute-done.5), channel_id=1, source_target_pairs={{0,4},{4,8},{8,12},{12,16},{16,20},{20,24},{24,28},{28,0},{1,5},{5... | collective-permute-start | bytes 3145736 | tf_op jit(solution)/shard_map/ppermute | solution.py:20
  239.4 4.0 copy-start.13
  454.1 12.4 copy-start.29
  454.1 12.5 %copy-start.26 = (f32[512,16,8]{0,2,1:T(8,128)S(1)}, f32[512,16,8]{0,2,1:T(8,128)}, u32[]{:S(2)}) copy-start(f32[512,16,8]{0,2,1:T(8,128)} %copy.107) | copy-start | bytes 786436
  554.0 11.7 copy-start.39
  565.7 5.3 copy-start.40
  582.8 6.7 copy-start.2
  589.5 297.9 %reduce-scatter.16.cloned.1.call-start = ((), (), s32[]{:S(2)}) async-start(), calls=%async_computation.18 | async-start | bytes 9437184 | tf_op jit(solution)/shard_map/reduce_scatter | solution.py:228
  598.8 5.8 copy-start.16
  604.6 325.1 %reduce-scatter.36.cloned.1.call-start = ((), (), s32[]{:S(2)}) async-start(), calls=%async_computation.30 | async-start | bytes 327680
  616.5 327.1 %reduce-scatter.20.cloned.1.call-start = ((), (), s32[]{:S(2)}) async-start(), calls=%async_computation.20 | async-start | bytes 2621440 | tf_op jit(solution)/shard_map/reduce_scatter | solution.py:267
  620.6 356.6 %reduce-scatter.26.cloned.1.call-start = ((), (), s32[]{:S(2)}) async-start(), calls=%async_computation.23 | async-start | bytes 2621440 | tf_op jit(solution)/shard_map/reduce_scatter | solution.py:276
  626.1 408.3 %reduce-scatter.28.cloned.1.call-start = ((), (), s32[]{:S(2)}) async-start(), calls=%async_computation.24 | async-start | bytes 7208960 | tf_op jit(solution)/shard_map/reduce_scatter | solution.py:279
  634.2 457.4 %reduce-scatter.30.cloned.1.call-start = ((), (), s32[]{:S(2)}) async-start(), calls=%async_computation.25 | async-start | bytes 7208960 | tf_op jit(solution)/shard_map/reduce_scatter | solution.py:282
  641.3 507.4 %reduce-scatter.32.cloned.1.call-start = ((), (), s32[]{:S(2)}) async-start(), calls=%async_computation.26 | async-start | bytes 7208960 | tf_op jit(solution)/shard_map/reduce_scatter | solution.py:285
  652.7 84.4 %copy-start.41 = (bf16[1,1024,1024]{2,1,0:T(8,128)(2,1)S(1)}, bf16[1,1024,1024]{2,1,0:T(8,128)(2,1)}, u32[]{:S(2)}) copy-start(bf16[1,1024,1024]{2,1,0:T(8,128)(2,1)} %all-gather.16.cloned.1.call-done) | copy-start | bytes 6291460
  652.8 518.9 %reduce-scatter.34.cloned.1.call-start = ((), (), s32[]{:S(2)}) async-start(), calls=%async_computation.29 | async-start | bytes 327680
  740.9 149.8 %copy-start.9 = (bf16[512,16,64]{0,2,1:T(8,128)(2,1)S(1)}, bf16[512,16,64]{0,2,1:T(8,128)(2,1)}, u32[]{:S(2)}) copy-start(bf16[512,16,64]{0,2,1:T(8,128)(2,1)} %multiply_convert_fusion.7) | copy-start | bytes 3145732
  890.7 4.2 copy-start.43
  894.9 310.5 %reduce-scatter.22.cloned.1.call-start = ((), (), s32[]{:S(2)}) async-start(), calls=%async_computation.21 | async-start | bytes 2621440 | tf_op jit(solution)/shard_map/reduce_scatter | solution.py:270
  897.8 341.2 %reduce-scatter.24.cloned.1.call-start = ((), (), s32[]{:S(2)}) async-start(), calls=%async_computation.22 | async-start | bytes 2621440 | tf_op jit(solution)/shard_map/reduce_scatter | solution.py:273
  1094.7 57.5 %copy-start.7 = (f32[512,1024]{1,0:T(8,128)S(1)}, f32[512,1024]{1,0:T(8,128)}, u32[]{:S(2)}) copy-start(f32[512,1024]{1,0:T(8,128)} %copy-done.5) | copy-start | bytes 6291460
  1094.7 57.5 %copy-start.30 = (f32[512]{0:T(512)S(1)}, f32[512]{0:T(512)}, u32[]{:S(2)}) copy-start(f32[512]{0:T(512)} %get-tuple-element.27) | copy-start | bytes 6148
  1094.7 57.5 %copy-start.32 = (pred[512]{0:T(512)(128)(4,1)S(1)}, pred[512]{0:T(512)(128)(4,1)}, u32[]{:S(2)}) copy-start(pred[512]{0:T(512)(128)(4,1)} %copy-done.31) | copy-start | bytes 1540
  1153.2 19.9 %collective-permute-start.8 = (f32[2,1024]{1,0:T(2,128)S(1)}, f32[2,1024]{1,0:T(2,128)S(1)}, u32[]{:S(2)}, u32[]{:S(2)}) collective-permute-start(f32[2,1024]{1,0:T(2,128)S(1)} %pad_add_fusion.1), channel_id=1, source_target_pairs={{1,0},{2,1},{3,2},{5,4},{6,5},{7,6},{9,8},{10,9},{11,10},{13,12},{... | collective-permute-start | bytes 24584 | tf_op jit(solution)/shard_map/ppermute | solution.py:35
  (27 other events, 56.2 us)
Sparse Core Ops, SparseCore 0:
  9.6 25.2 all-gather.13
  36.4 22.5 all-gather.15
  60.6 22.5 all-gather.11
  84.6 43.3 all-gather.23
  130.6 186.2 all-gather.27
  319.4 122.2 all-gather.25
  443.2 20.7 all-gather.17
  465.6 43.3 all-gather.21
  510.6 43.3 all-gather.19
  589.6 147.4 reduce-scatter.17
  740.7 146.5 reduce-scatter.15
  890.2 19.1 reduce-scatter.35
  912.5 31.1 reduce-scatter.19
  946.1 31.1 reduce-scatter.25
  979.6 54.7 reduce-scatter.27
  1036.8 54.7 reduce-scatter.29
  1093.9 54.7 reduce-scatter.31
  1151.6 20.0 reduce-scatter.33
  1174.2 31.1 reduce-scatter.21
  1207.8 31.1 reduce-scatter.23
